TPU v7x, 512 devices: a whole 4x8x8 slice. The times are simulated.
512 devices in a mesh: ax: 64 (over z, y_hi, x), rad: 8 (over y_lo, core).
Axes of the slice: x: 4, y: 8 (y_hi: 2, y_lo: 4; y = y_hi * 4 + y_lo), z: 8, core: 2. Of those that a mesh axis runs over, the one named last changes fastest.
Arguments:
- parcel_motion: float32 [6, 1048576], P(None, ('ax', 'rad')), may hold values from -6 to 6
- parcel_size: float32 [1048576], P(('ax', 'rad')), may hold values from 0.5 to 2
- parcel_block: int32 [16384], P(('ax', 'rad')), may hold values from 0 to 511, as said below
- parcel_offset: int32 [1048576], P(('ax', 'rad')), may hold values from 0 to 127
- gas_velocity: float32 [3, 1024, 4096], P(None, 'ax', 'rad'), may hold values from -6 to 6
- pressure: float32 [1024, 4096], P('ax', 'rad'), may hold values from -6 to 6
- block_cols: int32 [64, 512, 4], P('ax', 'rad'), may hold values from 0 to 511
- block_kinds: int32 [64, 512, 4], P('ax', 'rad'), may hold values from 0 to 7
- block_table: float32 [8, 128, 128], replicated, may hold values from -0.5 to 0.5
- send_axial: int32 [64, 8, 2, 64], P('ax', 'rad'), may hold values from 0 to 2047, as said below
- send_radial: int32 [64, 8, 2, 32], P('ax', 'rad'), may hold values from 0 to 2047, as said below
- send_counts: int32 [64, 8, 4], P('ax', 'rad'), may hold values from 0 to 64, as said below
Outputs:
- motion_out: float32 [6, 1048576], P(None, ('ax', 'rad'))
- arrivals_axial: float32 [64, 8, 2, 7, 64], P('ax', 'rad')
- arrivals_radial: float32 [64, 8, 2, 7, 32], P('ax', 'rad')
- gas_out: float32 [3, 1024, 4096], P(None, 'ax', 'rad')
- liquid_load: float32 [1024, 4096], P('ax', 'rad')
- pressure_image: float32 [1024, 4096], P('ax', 'rad')
Inputs may be any that keep to these rules, and one draw needn't show every extreme that they name: `parcel_block`: most of a device's parcel blocks lie in cell blocks of its own radial group; the others lie in other radial groups of the slab. `send_axial`: each device's lists (both axial and both radial together) hold distinct indices of that device's parcels; entries past the counts are unused. `send_radial`: disjoint from the device's axial lists, see send_axial. `send_counts`: axial counts are at most 64, radial ones at most 32; devices of radial group 0 send full lists in all four directions.
All inputs are finite; a program needn't handle non-finite values.
Results may differ from a plain program's by a relative error of at most 0.000084.
Values sent between devices are 32-bit elements; how exact they have to be, the bound alone decides.
A program may use at most 64 MiB of HBM per device.

v0:
```python
import jax
import jax.numpy as jnp
from jax import lax
from jax.sharding import PartitionSpec as P

BLOCK = 128
PARCEL_GROUP = 64
NT = 8
TOP_PRECISION = lax.Precision.HIGHEST
DRAG = 0.5
STEP = 0.5
DIAG = 6.0


def from_behind(value, axis, steps):
    count = lax.axis_size(axis)
    leading, last = (max(0, -steps), min(count, count - steps))
    return lax.ppermute(value, axis, [(source, source + steps) for source in range(leading, last)])


def with_halo(x, sides, width):
    for axis, dim in sides:
        count, length = (lax.axis_size(axis), x.shape[dim])
        up = [(i, (i + 1) % count) for i in range(count - 1)]
        down = [(j, i) for i, j in up]
        last = lax.slice_in_dim(x, length - width, length, axis=dim)
        leading = lax.slice_in_dim(x, 0, width, axis=dim)
        before = lax.ppermute(last, axis, up)
        after = lax.ppermute(leading, axis, down)
        x = jnp.concatenate([before, x, after], axis=dim)
    return x


def pass_axial(payload, offset):
    return from_behind(payload, "ax", offset)


def pass_radial(payload, offset):
    return from_behind(payload, "rad", offset)


def on_device(
    parcel_motion,
    parcel_size,
    parcel_block,
    parcel_offset,
    gas_velocity,
    pressure,
    block_cols,
    block_kinds,
    block_table,
    send_axial,
    send_radial,
    send_counts,
):
    blocks_here = pressure.shape[0] * pressure.shape[1] // BLOCK
    gas_local = gas_velocity.reshape(3, blocks_here, BLOCK)
    pres_local = pressure.reshape(blocks_here, BLOCK)
    parcel_groups = parcel_block.shape[0]
    gas_slab, pres_slab = (
        lax.all_gather(gas_local, "rad", axis=1, tiled=True),
        lax.all_gather(pres_local, "rad", axis=0, tiled=True),
    )
    gas_lookup = gas_slab[:, parcel_block, :]
    offsets = parcel_offset.reshape(parcel_groups, PARCEL_GROUP)
    block_selector = (offsets[:, :, None] == jnp.arange(BLOCK, dtype=jnp.int32)).astype(jnp.float32)
    visited_flags = jnp.einsum(
        "fpm,pkm->fpk", gas_lookup, block_selector, precision=TOP_PRECISION
    ).reshape(3, parcel_groups * PARCEL_GROUP)
    velocity = parcel_motion[3:6]
    factor = jnp.exp(-DRAG / (parcel_size * parcel_size))
    new_vel = visited_flags + (velocity - visited_flags) * factor
    new_pos = parcel_motion[0:3] + STEP * new_vel
    motion_out = jnp.concatenate([new_pos, new_vel], axis=0)
    mass = parcel_size * parcel_size * parcel_size
    deposit = jnp.concatenate([-mass * (new_vel - velocity), mass[None]], axis=0)
    deposit = deposit.reshape(4, parcel_groups, PARCEL_GROUP)
    dep_flat = jnp.einsum("cbj,bjn->bcn", deposit, block_selector, precision=TOP_PRECISION).reshape(
        parcel_groups, 4 * BLOCK
    )
    rows_here = jnp.arange(blocks_here * lax.axis_size("rad"), dtype=jnp.int32)
    hits = (parcel_block[None, :] == rows_here[:, None]).astype(jnp.float32)
    summed = lax.psum_scatter(
        jnp.dot(hits, dep_flat, precision=TOP_PRECISION), "rad", scatter_dimension=0, tiled=True
    )
    sources = summed.reshape(blocks_here, 4, BLOCK).transpose(1, 0, 2)
    gas_out = gas_velocity + sources[:3].reshape(gas_velocity.shape)
    liquid_load = sources[3].reshape(pressure.shape)
    state = jnp.concatenate([motion_out, parcel_size[None]], axis=0)
    counts = send_counts[0, 0]

    def pack(lists, live_counts):
        taken = jnp.moveaxis(jnp.take(state, lists, axis=1), 1, 0)
        live = jnp.arange(lists.shape[1], dtype=jnp.int32)[None, :] < live_counts[:, None]
        return jnp.where(live[:, None, :], taken, jnp.float32(0.0))

    out_ax = pack(send_axial[0, 0], counts[0:2])
    arrivals_axial = jnp.stack([pass_axial(out_ax[0], 1), pass_axial(out_ax[1], -1)], axis=0)[
        None, None
    ]
    out_rad = pack(send_radial[0, 0], counts[2:4])
    arrivals_radial = jnp.stack([pass_radial(out_rad[0], 1), pass_radial(out_rad[1], -1)], axis=0)[
        None, None
    ]
    padded = with_halo(pressure, (("ax", 0),), 1)
    image = DIAG * pressure - padded[2:] - padded[:-2]
    picked = pres_slab[block_cols[0]]
    kinds = (block_kinds[0][..., None] == jnp.arange(NT, dtype=jnp.int32)).astype(jnp.float32)
    grouped = jnp.einsum("bkt,bkn->btn", kinds, picked, precision=TOP_PRECISION)
    coupled = jnp.einsum("btn,tmn->bm", grouped, block_table, precision=TOP_PRECISION)
    pressure_image = image + coupled.reshape(pressure.shape)
    return (motion_out, arrivals_axial, arrivals_radial, gas_out, liquid_load, pressure_image)


def solution(mesh):
    return jax.shard_map(
        on_device,
        mesh=mesh,
        in_specs=(
            P(None, ("ax", "rad")),
            P(("ax", "rad")),
            P(("ax", "rad")),
            P(("ax", "rad")),
            P(None, "ax", "rad"),
            P("ax", "rad"),
            P("ax", "rad", None),
            P("ax", "rad", None),
            P(),
            P("ax", "rad", None, None),
            P("ax", "rad", None, None),
            P("ax", "rad", None),
        ),
        out_specs=(
            P(None, ("ax", "rad")),
            P("ax", "rad", None, None, None),
            P("ax", "rad", None, None, None),
            P(None, "ax", "rad"),
            P("ax", "rad"),
            P("ax", "rad"),
        ),
        check_vma=False,
    )
```

profile of v0, /device:TPU:264, one launch (start us, length us, event | category | flops | bytes accessed | tf_op | source)
XLA Modules:
  0.0 99.1 jit_solution(3269439988784230751)
XLA Ops:
  7.2 0.8 multiply_multiply_fusion
  8.1 0.9 reshape.182
  9.0 15.8 %all_gather.6 = f32[3,512,128]{2,1,0:T(8,128)S(1)} all-gather(f32[3,64,128]{2,1,0:T(8,128)S(1)} %reshape.182), channel_id=1, replica_groups=mesh['ax'=64,'rad'=8] {'rad'}, dimensions={1}, use_global_device_ids=true | all-gather | bytes 884736 | tf_op jit(solution)/shard_map/all_gather | solution.py:61
  25.4 0.6 gather_fusion
  26.0 1.0 convolution_bitcast_fusion
  27.1 0.7 copy-done.3
  27.9 0.7 copy-done.4
  29.4 0.6 gather_fusion.2
  30.1 0.6 copy-done.10
  30.8 2.3 %collective-permute-start.2 = (f32[7,32]{1,0:T(8,128)S(1)}, f32[7,32]{1,0:T(8,128)S(1)}, u32[]{:S(2)}, u32[]{:S(2)}) collective-permute-start(f32[7,32]{1,0:T(8,128)S(1)} %get-tuple-element.31), channel_id=1, source_target_pairs={{0,1},{1,2},{2,3},{3,4},{4,5},{5,6},{6,7},{8,9},{9,10},{10,11},{11... | collective-permute-start | bytes 2696 | tf_op jit(solution)/shard_map/ppermute | solution.py:18
  33.1 3.3 %collective-permute-start.3 = (f32[7,32]{1,0:T(8,128)S(1)}, f32[7,32]{1,0:T(8,128)S(1)}, u32[]{:S(2)}, u32[]{:S(2)}) collective-permute-start(f32[7,32]{1,0:T(8,128)S(1)} %get-tuple-element.32), channel_id=1, source_target_pairs={{1,0},{2,1},{3,2},{4,3},{5,4},{6,5},{7,6},{9,8},{10,9},{11,10},{12... | collective-permute-start | bytes 2696 | tf_op jit(solution)/shard_map/ppermute | solution.py:18
  36.6 0.7 fusion
  37.3 1.6 %fusion.4 = f32[512,512]{1,0:T(8,128)} fusion(s32[32]{0:T(128)S(1)} %copy-done.11, f32[4,8,4,128]{3,2,1,0:T(4,128)S(1)} %bitcast.62), kind=kOutput, calls=%fused_computation.12 | convolution fusion | flops 100679680 | bytes 1114240 | tf_op jit(solution)/shard_map/dot_general | solution.py:84
  38.9 0.7 copy-done.7
  39.7 0.6 gather_fusion.1
  40.5 3.4 %collective-permute-start = (f32[7,64]{1,0:T(8,128)S(1)}, f32[7,64]{1,0:T(8,128)S(1)}, u32[]{:S(2)}, u32[]{:S(2)}) collective-permute-start(f32[7,64]{1,0:T(8,128)S(1)} %get-tuple-element.33), channel_id=1, source_target_pairs={{0,8},{8,16},{16,24},{24,32},{32,40},{40,48},{48,56},{56,64},{64,7... | collective-permute-start | bytes 5384 | tf_op jit(solution)/shard_map/ppermute | solution.py:18
  43.9 10.6 %collective-permute-start.1 = (f32[7,64]{1,0:T(8,128)S(1)}, f32[7,64]{1,0:T(8,128)S(1)}, u32[]{:S(2)}, u32[]{:S(2)}) collective-permute-start(f32[7,64]{1,0:T(8,128)S(1)} %get-tuple-element.34), channel_id=1, source_target_pairs={{8,0},{16,8},{24,16},{32,24},{40,32},{48,40},{56,48},{64,56},{72,6... | collective-permute-start | bytes 5384 | tf_op jit(solution)/shard_map/ppermute | solution.py:18
  54.5 1.9 %collective-permute-start.4 = (f32[1,512]{1,0:T(1,128)S(1)}, f32[1,512]{1,0:T(1,128)S(1)}, u32[]{:S(2)}, u32[]{:S(2)}) collective-permute-start(f32[1,512]{1,0:T(1,128)S(1)} %get-tuple-element.26), channel_id=1, source_target_pairs={{8,0},{16,8},{24,16},{32,24},{40,32},{48,40},{56,48},{64,56},{72,6... | collective-permute-start | bytes 6152 | tf_op jit(solution)/shard_map/ppermute | solution.py:29
  57.2 14.9 %all_gather.7 = f32[512,128]{1,0:T(8,128)S(1)} all-gather(f32[64,128]{1,0:T(8,128)S(1)} %reshape.187), channel_id=1, replica_groups=mesh['ax'=64,'rad'=8] {'rad'}, dimensions={0}, use_global_device_ids=true | all-gather | bytes 294912 | tf_op jit(solution)/shard_map/all_gather | solution.py:62
  72.1 0.7 gather_fusion.3
  72.9 0.6 pad_maximum_fusion
  73.5 0.6 fusion.6
  74.1 0.7 convolution_bitcast_fusion.1
  74.8 3.6 %collective-permute-start.5 = (f32[1,512]{1,0:T(1,128)S(1)}, f32[1,512]{1,0:T(1,128)S(1)}, u32[]{:S(2)}, u32[]{:S(2)}) collective-permute-start(f32[1,512]{1,0:T(1,128)S(1)} %get-tuple-element.27), channel_id=1, source_target_pairs={{0,8},{8,16},{16,24},{24,32},{32,40},{40,48},{48,56},{56,64},{64,7... | collective-permute-start | bytes 6152 | tf_op jit(solution)/shard_map/ppermute | solution.py:28
  78.4 0.6 maximum_bitcast_fusion.1
  79.1 0.6 maximum_bitcast_fusion
  79.7 8.7 %collective-permute-done.5 = f32[1,512]{1,0:T(1,128)S(1)} collective-permute-done((f32[1,512]{1,0:T(1,128)S(1)}, f32[1,512]{1,0:T(1,128)S(1)}, u32[]{:S(2)}, u32[]{:S(2)}) %collective-permute-start.5) | collective-permute-done | bytes 2080 | tf_op jit(solution)/shard_map/ppermute | solution.py:28
  88.4 0.6 fusion.15
  89.1 0.9 reshape.185
  90.2 0.9 copy-done.1
  91.0 0.7 add.87
  91.7 0.6 reshape_squeeze.3
  (70 shorter events, 3.4 us)
Async XLA Ops:
  7.2 67.0 %copy-start = (f32[8,128,128]{2,1,0:T(8,128)S(1)}, f32[8,128,128]{2,1,0:T(8,128)}, u32[]{:S(2)}) copy-start(f32[8,128,128]{2,1,0:T(8,128)} %param.20) | copy-start | bytes 1572868
  7.2 0.8 copy-start.5
  7.2 81.9 %reduce-scatter.2.cloned.1.call-start = ((), (), s32[]{:S(2)}) async-start(), calls=%async_computation.1 | async-start | bytes 1179648 | tf_op jit(solution)/shard_map/reduce_scatter | solution.py:83
  24.8 0.7 copy-start.11
  27.0 0.9 copy-start.3
  27.9 0.7 copy-start.4
  28.6 0.7 copy-start.6
  30.0 0.7 copy-start.10
  30.8 44.0 %collective-permute-start.2 = (f32[7,32]{1,0:T(8,128)S(1)}, f32[7,32]{1,0:T(8,128)S(1)}, u32[]{:S(2)}, u32[]{:S(2)}) collective-permute-start(f32[7,32]{1,0:T(8,128)S(1)} %get-tuple-element.31), channel_id=1, source_target_pairs={{0,1},{1,2},{2,3},{3,4},{4,5},{5,6},{6,7},{8,9},{9,10},{10,11},{11... | collective-permute-start | bytes 2696 | tf_op jit(solution)/shard_map/ppermute | solution.py:18
  33.1 45.3 %collective-permute-start.3 = (f32[7,32]{1,0:T(8,128)S(1)}, f32[7,32]{1,0:T(8,128)S(1)}, u32[]{:S(2)}, u32[]{:S(2)}) collective-permute-start(f32[7,32]{1,0:T(8,128)S(1)} %get-tuple-element.32), channel_id=1, source_target_pairs={{1,0},{2,1},{3,2},{4,3},{5,4},{6,5},{7,6},{9,8},{10,9},{11,10},{12... | collective-permute-start | bytes 2696 | tf_op jit(solution)/shard_map/ppermute | solution.py:18
  38.9 0.7 copy-start.7
  40.4 14.1 %copy-start.2 = (f32[16,512]{1,0:T(8,128)S(1)}, f32[16,512]{1,0:T(8,128)}, u32[]{:S(2)}) copy-start(f32[16,512]{1,0:T(8,128)} %param.17) | copy-start | bytes 98308
  40.5 38.5 %collective-permute-start = (f32[7,64]{1,0:T(8,128)S(1)}, f32[7,64]{1,0:T(8,128)S(1)}, u32[]{:S(2)}, u32[]{:S(2)}) collective-permute-start(f32[7,64]{1,0:T(8,128)S(1)} %get-tuple-element.33), channel_id=1, source_target_pairs={{0,8},{8,16},{16,24},{24,32},{32,40},{40,48},{48,56},{56,64},{64,7... | collective-permute-start | bytes 5384 | tf_op jit(solution)/shard_map/ppermute | solution.py:18
  43.9 35.1 %collective-permute-start.1 = (f32[7,64]{1,0:T(8,128)S(1)}, f32[7,64]{1,0:T(8,128)S(1)}, u32[]{:S(2)}, u32[]{:S(2)}) collective-permute-start(f32[7,64]{1,0:T(8,128)S(1)} %get-tuple-element.34), channel_id=1, source_target_pairs={{8,0},{16,8},{24,16},{32,24},{40,32},{48,40},{56,48},{64,56},{72,6... | collective-permute-start | bytes 5384 | tf_op jit(solution)/shard_map/ppermute | solution.py:18
  54.5 2.0 %copy-start.9 = (s32[1,64,4]{1,2,0:T(4,128)S(1)}, s32[1,64,4]{1,2,0:T(4,128)}, u32[]{:S(2)}) copy-start(s32[1,64,4]{1,2,0:T(4,128)} %param.18) | copy-start | bytes 3076
  54.5 25.2 %collective-permute-start.4 = (f32[1,512]{1,0:T(1,128)S(1)}, f32[1,512]{1,0:T(1,128)S(1)}, u32[]{:S(2)}, u32[]{:S(2)}) collective-permute-start(f32[1,512]{1,0:T(1,128)S(1)} %get-tuple-element.26), channel_id=1, source_target_pairs={{8,0},{16,8},{24,16},{32,24},{40,32},{48,40},{56,48},{64,56},{72,6... | collective-permute-start | bytes 6152 | tf_op jit(solution)/shard_map/ppermute | solution.py:29
  56.4 0.7 copy-start.8
  74.8 13.6 %collective-permute-start.5 = (f32[1,512]{1,0:T(1,128)S(1)}, f32[1,512]{1,0:T(1,128)S(1)}, u32[]{:S(2)}, u32[]{:S(2)}) collective-permute-start(f32[1,512]{1,0:T(1,128)S(1)} %get-tuple-element.27), channel_id=1, source_target_pairs={{0,8},{8,16},{16,24},{24,32},{32,40},{40,48},{48,56},{56,64},{64,7... | collective-permute-start | bytes 6152 | tf_op jit(solution)/shard_map/ppermute | solution.py:28
  90.1 0.9 copy-start.1
Sparse Core Ops, SparseCore 0:
  39.0 37.2 reduce-scatter.1
where the time goes:
time: 99.7 us; the launch traced here: 99.1 us
  blocking collectives  30.7 us (31%)
  starting transfers between devices  25.1 us (25%)
  between operations  14.3 us (14%)
  local copies, waits for them, and re-layouts  11.6 us (12%)
  waiting for transfers between devices  8.78 us (9%)
  matrix products  4.54 us (5%)
  other arithmetic  4.18 us (4%)
    ppermute x4, starting transfers between devices, from_behind(): lax.ppermute(value, axis, [(source, source + steps) for source in range(l...  19.5 us
    all_gather x1, blocking collectives, on_device(): lax.all_gather(gas_local, 'rad', axis=1, tiled=True)  15.8 us
    all_gather x1, blocking collectives, on_device(): lax.all_gather(pres_local, 'rad', axis=0, tiled=True)  14.9 us
    ppermute x1, waiting for transfers between devices, with_halo(): before = lax.ppermute(last, axis, up)  8.75 us
    unnamed x24, local copies, waits for them, and re-layouts  4.38 us
    ppermute x1, starting transfers between devices, with_halo(): before = lax.ppermute(last, axis, up)  3.57 us
  transfers between devices with their start and end apart: 7, of which 1 were waited for; matrix products, arithmetic and copies ran while one was open for 8% of the time, Pallas kernels for 0%

commit v1 on v0

--- a/solution.py
+++ b/solution.py
@@ -59,7 +59,9 @@
     parcel_groups = parcel_block.shape[0]
     gas_slab, pres_slab = (
         lax.all_gather(gas_local, "rad", axis=1, tiled=True),
-        lax.all_gather(pres_local, "rad", axis=0, tiled=True),
+        jnp.concatenate(
+            lax.all_to_all(jnp.stack([pres_local] * lax.axis_size("rad")), "rad", 0, 0), axis=0
+        ),
     )
     gas_lookup = gas_slab[:, parcel_block, :]
     offsets = parcel_offset.reshape(parcel_groups, PARCEL_GROUP)

time: 99.7 us -> 95 us (0.953)
  the two profiles are of different devices: /device:TPU:264 before, /device:TPU:6 now
where the time goes in v1:
time: 95 us; the launch traced here: 94.3 us
  starting transfers between devices  29.1 us (31%)
  blocking collectives  15.8 us (17%)
  waiting for transfers between devices  14.6 us (15%)
  between operations  14.4 us (15%)
  local copies, waits for them, and re-layouts  11.9 us (13%)
  matrix products  4.56 us (5%)
  other arithmetic  4.18 us (4%)
    all_gather x1, blocking collectives, on_device(): lax.all_gather(gas_local, 'rad', axis=1, tiled=True)  15.8 us
    reduce_scatter x1, waiting for transfers between devices, on_device(): lax.psum_scatter(jnp.dot(hits, dep_flat, precision=TOP_PRECISION), 'rad',...  14.3 us
    ppermute x4, starting transfers between devices, from_behind(): lax.ppermute(value, axis, [(source, source + steps) for source in range(l...  13 us
    ppermute x1, starting transfers between devices, with_halo(): before = lax.ppermute(last, axis, up)  9.94 us
    all_to_all x1, starting transfers between devices, on_device(): lax.all_to_all(jnp.stack([pres_local] * lax.axis_size('rad')), 'rad', 0, 0)  4.12 us
    unnamed x24, local copies, waits for them, and re-layouts  3.97 us
    ppermute x1, starting transfers between devices, with_halo(): after = lax.ppermute(leading, axis, down)  1.92 us
  transfers between devices with their start and end apart: 8, of which 2 were waited for; matrix products, arithmetic and copies ran while one was open for 9% of the time, Pallas kernels for 0%

profile of v1, /device:TPU:6, one launch (start us, length us, event | category | flops | bytes accessed | tf_op | source)
XLA Modules:
  0.0 94.3 jit_solution(17302884043642863849)
XLA Ops:
  7.2 0.8 multiply_multiply_fusion
  8.1 0.9 reshape.184
  9.0 15.8 %all_gather.3 = f32[3,512,128]{2,1,0:T(8,128)S(1)} all-gather(f32[3,64,128]{2,1,0:T(8,128)S(1)} %reshape.184), channel_id=1, replica_groups=mesh['ax'=64,'rad'=8] {'rad'}, dimensions={1}, use_global_device_ids=true | all-gather | bytes 884736 | tf_op jit(solution)/shard_map/all_gather | solution.py:61
  25.4 0.6 gather_fusion
  26.0 1.0 %convolution_bitcast_fusion = f32[3,32,64]{2,0,1:T(4,128)S(1)} fusion(s32[32,64]{1,0:T(8,128)S(1)} %eq.43, f32[32,3,128]{2,1,0:T(4,128)S(1)} %gather_fusion), kind=kOutput, calls=%fused_computation.4 | convolution fusion | flops 9699328 | bytes 81920 | tf_op jit(solution)/shard_map/fpm,pkm->fpk/dot_general | solution.py:69
  27.1 0.7 copy-done.3
  27.9 0.7 copy-done.4
  29.4 0.6 gather_fusion.2
  30.8 2.2 %collective-permute-start.2 = (f32[7,32]{1,0:T(8,128)S(1)}, f32[7,32]{1,0:T(8,128)S(1)}, u32[]{:S(2)}, u32[]{:S(2)}) collective-permute-start(f32[7,32]{1,0:T(8,128)S(1)} %get-tuple-element.31), channel_id=1, source_target_pairs={{0,1},{1,2},{2,3},{3,4},{4,5},{5,6},{6,7},{8,9},{9,10},{10,11},{11... | collective-permute-start | bytes 2696 | tf_op jit(solution)/shard_map/ppermute | solution.py:18
  33.1 1.3 %collective-permute-start.3 = (f32[7,32]{1,0:T(8,128)S(1)}, f32[7,32]{1,0:T(8,128)S(1)}, u32[]{:S(2)}, u32[]{:S(2)}) collective-permute-start(f32[7,32]{1,0:T(8,128)S(1)} %get-tuple-element.32), channel_id=1, source_target_pairs={{1,0},{2,1},{3,2},{4,3},{5,4},{6,5},{7,6},{9,8},{10,9},{11,10},{12... | collective-permute-start | bytes 2696 | tf_op jit(solution)/shard_map/ppermute | solution.py:18
  34.6 0.7 fusion
  35.3 1.6 %fusion.4 = f32[512,512]{1,0:T(8,128)} fusion(s32[32]{0:T(128)S(1)} %copy-done.11, f32[4,8,4,128]{3,2,1,0:T(4,128)S(1)} %bitcast.64), kind=kOutput, calls=%fused_computation.12 | convolution fusion | flops 100679680 | bytes 1114240 | tf_op jit(solution)/shard_map/dot_general | solution.py:86
  36.9 0.7 copy-done.7
  37.7 0.6 gather_fusion.1
  38.5 7.6 %collective-permute-start = (f32[7,64]{1,0:T(8,128)S(1)}, f32[7,64]{1,0:T(8,128)S(1)}, u32[]{:S(2)}, u32[]{:S(2)}) collective-permute-start(f32[7,64]{1,0:T(8,128)S(1)} %get-tuple-element.33), channel_id=1, source_target_pairs={{0,8},{8,16},{16,24},{24,32},{32,40},{40,48},{48,56},{56,64},{64,7... | collective-permute-start | bytes 5384 | tf_op jit(solution)/shard_map/ppermute | solution.py:18
  46.1 1.9 %collective-permute-start.1 = (f32[7,64]{1,0:T(8,128)S(1)}, f32[7,64]{1,0:T(8,128)S(1)}, u32[]{:S(2)}, u32[]{:S(2)}) collective-permute-start(f32[7,64]{1,0:T(8,128)S(1)} %get-tuple-element.34), channel_id=1, source_target_pairs={{8,0},{16,8},{24,16},{32,24},{40,32},{48,40},{56,48},{64,56},{72,6... | collective-permute-start | bytes 5384 | tf_op jit(solution)/shard_map/ppermute | solution.py:18
  48.0 1.9 %collective-permute-start.4 = (f32[1,512]{1,0:T(1,128)S(1)}, f32[1,512]{1,0:T(1,128)S(1)}, u32[]{:S(2)}, u32[]{:S(2)}) collective-permute-start(f32[1,512]{1,0:T(1,128)S(1)} %get-tuple-element.26), channel_id=1, source_target_pairs={{8,0},{16,8},{24,16},{32,24},{40,32},{48,40},{56,48},{64,56},{72,6... | collective-permute-start | bytes 6152 | tf_op jit(solution)/shard_map/ppermute | solution.py:29
  50.0 0.7 stack.27
  50.7 4.1 %all-to-all-start = ((f32[8,64,128]{2,1,0:T(8,128)}), f32[8,64,128]{2,1,0:T(8,128)S(1)}, u32[]{:S(2)}, u32[]{:S(2)}) async-start(f32[8,64,128]{2,1,0:T(8,128)} %stack.27), calls=%async_computation.1 | async-start | bytes 524288 | tf_op jit(solution)/shard_map/all_to_all | solution.py:63
  55.0 0.6 pad_maximum_fusion
  55.8 9.9 %collective-permute-start.5 = (f32[1,512]{1,0:T(1,128)S(1)}, f32[1,512]{1,0:T(1,128)S(1)}, u32[]{:S(2)}, u32[]{:S(2)}) collective-permute-start(f32[1,512]{1,0:T(1,128)S(1)} %get-tuple-element.27), channel_id=1, source_target_pairs={{0,8},{8,16},{16,24},{24,32},{32,40},{40,48},{48,56},{56,64},{64,7... | collective-permute-start | bytes 6152 | tf_op jit(solution)/shard_map/ppermute | solution.py:28
  65.8 0.6 maximum_bitcast_fusion.1
  66.4 0.6 maximum_bitcast_fusion
  67.3 0.7 gather_fusion.3
  68.0 0.6 fusion.6
  68.6 0.7 convolution_bitcast_fusion.1
  69.4 0.6 fusion.15
  70.0 14.3 %reduce-scatter.2.cloned.1.call-done = f32[64,512]{1,0:T(8,128)} async-done(((f32[512,512]{1,0:T(8,128)}), f32[64,512]{1,0:T(8,128)}) %reduce-scatter.2.cloned.1.call-update) | async-done | bytes 131088 | tf_op jit(solution)/shard_map/reduce_scatter | solution.py:85
  84.2 0.9 %reshape.187 = f32[64,4,128]{2,1,0:T(4,128)S(1)} reshape(f32[64,512]{1,0:T(8,128)} %reduce-scatter.2.cloned.1.call-done) | data formatting | bytes 262144 | tf_op jit(solution)/shard_map/reshape | solution.py:88
  85.3 0.9 copy-done.1
  86.2 0.7 add.87
  86.9 0.6 reshape_squeeze.3
  (72 shorter events, 3.8 us)
Async XLA Ops:
  7.2 61.5 %copy-start = (f32[8,128,128]{2,1,0:T(8,128)S(1)}, f32[8,128,128]{2,1,0:T(8,128)}, u32[]{:S(2)}) copy-start(f32[8,128,128]{2,1,0:T(8,128)} %param.20) | copy-start | bytes 1572868
  7.2 0.8 copy-start.5
  7.2 77.0 %reduce-scatter.2.cloned.1.call-start = ((), (), s32[]{:S(2)}) async-start(), calls=%async_computation.2 | async-start | bytes 1179648 | tf_op jit(solution)/shard_map/reduce_scatter | solution.py:85
  24.7 0.7 copy-start.11
  27.0 0.9 copy-start.3
  27.9 0.7 copy-start.4
  28.6 0.7 copy-start.6
  30.0 0.7 copy-start.10
  30.8 25.0 %collective-permute-start.2 = (f32[7,32]{1,0:T(8,128)S(1)}, f32[7,32]{1,0:T(8,128)S(1)}, u32[]{:S(2)}, u32[]{:S(2)}) collective-permute-start(f32[7,32]{1,0:T(8,128)S(1)} %get-tuple-element.31), channel_id=1, source_target_pairs={{0,1},{1,2},{2,3},{3,4},{4,5},{5,6},{6,7},{8,9},{9,10},{10,11},{11... | collective-permute-start | bytes 2696 | tf_op jit(solution)/shard_map/ppermute | solution.py:18
  33.1 32.7 %collective-permute-start.3 = (f32[7,32]{1,0:T(8,128)S(1)}, f32[7,32]{1,0:T(8,128)S(1)}, u32[]{:S(2)}, u32[]{:S(2)}) collective-permute-start(f32[7,32]{1,0:T(8,128)S(1)} %get-tuple-element.32), channel_id=1, source_target_pairs={{1,0},{2,1},{3,2},{4,3},{5,4},{6,5},{7,6},{9,8},{10,9},{11,10},{12... | collective-permute-start | bytes 2696 | tf_op jit(solution)/shard_map/ppermute | solution.py:18
  36.9 0.7 copy-start.7
  38.4 9.5 %copy-start.2 = (f32[16,512]{1,0:T(8,128)S(1)}, f32[16,512]{1,0:T(8,128)}, u32[]{:S(2)}) copy-start(f32[16,512]{1,0:T(8,128)} %param.17) | copy-start | bytes 98308
  38.5 27.9 %collective-permute-start = (f32[7,64]{1,0:T(8,128)S(1)}, f32[7,64]{1,0:T(8,128)S(1)}, u32[]{:S(2)}, u32[]{:S(2)}) collective-permute-start(f32[7,64]{1,0:T(8,128)S(1)} %get-tuple-element.33), channel_id=1, source_target_pairs={{0,8},{8,16},{16,24},{24,32},{32,40},{40,48},{48,56},{56,64},{64,7... | collective-permute-start | bytes 5384 | tf_op jit(solution)/shard_map/ppermute | solution.py:18
  46.1 20.3 %collective-permute-start.1 = (f32[7,64]{1,0:T(8,128)S(1)}, f32[7,64]{1,0:T(8,128)S(1)}, u32[]{:S(2)}, u32[]{:S(2)}) collective-permute-start(f32[7,64]{1,0:T(8,128)S(1)} %get-tuple-element.34), channel_id=1, source_target_pairs={{8,0},{16,8},{24,16},{32,24},{40,32},{48,40},{56,48},{64,56},{72,6... | collective-permute-start | bytes 5384 | tf_op jit(solution)/shard_map/ppermute | solution.py:18
  48.0 21.3 %collective-permute-start.4 = (f32[1,512]{1,0:T(1,128)S(1)}, f32[1,512]{1,0:T(1,128)S(1)}, u32[]{:S(2)}, u32[]{:S(2)}) collective-permute-start(f32[1,512]{1,0:T(1,128)S(1)} %get-tuple-element.26), channel_id=1, source_target_pairs={{8,0},{16,8},{24,16},{32,24},{40,32},{48,40},{56,48},{64,56},{72,6... | collective-permute-start | bytes 6152 | tf_op jit(solution)/shard_map/ppermute | solution.py:29
  50.7 4.1 %copy-start.9 = (s32[1,64,4]{1,2,0:T(4,128)S(1)}, s32[1,64,4]{1,2,0:T(4,128)}, u32[]{:S(2)}) copy-start(s32[1,64,4]{1,2,0:T(4,128)} %param.18) | copy-start | bytes 3076
  50.7 16.6 %all-to-all-start = ((f32[8,64,128]{2,1,0:T(8,128)}), f32[8,64,128]{2,1,0:T(8,128)S(1)}, u32[]{:S(2)}, u32[]{:S(2)}) async-start(f32[8,64,128]{2,1,0:T(8,128)} %stack.27), calls=%async_computation.1 | async-start | bytes 524288 | tf_op jit(solution)/shard_map/all_to_all | solution.py:63
  55.0 0.7 copy-start.8
  55.8 13.5 %collective-permute-start.5 = (f32[1,512]{1,0:T(1,128)S(1)}, f32[1,512]{1,0:T(1,128)S(1)}, u32[]{:S(2)}, u32[]{:S(2)}) collective-permute-start(f32[1,512]{1,0:T(1,128)S(1)} %get-tuple-element.27), channel_id=1, source_target_pairs={{0,8},{8,16},{16,24},{24,32},{32,40},{40,48},{48,56},{56,64},{64,7... | collective-permute-start | bytes 6152 | tf_op jit(solution)/shard_map/ppermute | solution.py:28
  85.3 0.9 copy-start.1
Sparse Core Ops, SparseCore 0:
  37.0 47.1 reduce-scatter.1
